TPU v7x, 256 devices: a whole 4x4x8 slice. The times are simulated.
256 devices in a mesh: pipe: 8 (over x_lo, y), expert: 32 (over z, x_hi, core).
Axes of the slice: x: 4 (x_hi: 2, x_lo: 2; x = x_hi * 2 + x_lo), y: 4, z: 8, core: 2. Of those that a mesh axis runs over, the one named last changes fastest.
Arguments:
- tokens: bfloat16 [8, 4096, 2048], P('pipe', 'expert'), may hold values from -6 to 6
- routes: int32 [8, 4096, 6], P('pipe', 'expert'), may hold values from 0 to 31, all different within a row; in each aligned block of 128 rows (0 to 127, 128 to 255, ..., all dimensions but the last counted through in order) at most 36 rows name the same one
- norm_gain: float32 [8, 2048], P('pipe'), may hold values from 0.1 to 1.9
- router_weight: bfloat16 [8, 2048, 32], P('pipe'), may hold values from -0.125 to 0.125
- w_gate: bfloat16 [8, 32, 2048, 768], P('pipe', 'expert'), may hold values from -0.125 to 0.125
- w_up: bfloat16 [8, 32, 2048, 768], P('pipe', 'expert'), may hold values from -0.125 to 0.125
- w_down: bfloat16 [8, 32, 768, 2048], P('pipe', 'expert'), may hold values from -0.21875 to 0.21875
Outputs:
- received: bfloat16 [8, 4096, 2048], P('pipe', 'expert')
Inputs may be any that keep to these rules, and one draw needn't show every extreme that they name: Within each aligned block of 128 tokens of a section (the tokens of one device), the 6 routes of a token name different experts and no expert is named by more than 36 routes; some expert is named by exactly 36 routes in some block; every expert is named somewhere.
All inputs are finite; a program needn't handle non-finite values.
Results may differ from a plain program's by a relative error of at most 0.0039.
Values may be sent and summed in bfloat16 or wider, within the bound.
A program may use at most 128 MiB of HBM per device.

v0:
```python
import jax
import jax.numpy as jnp
from jax import lax
from jax.sharding import PartitionSpec as P


def shifted(shard, axis, by):
    devices = lax.axis_size(axis)
    return lax.ppermute(shard, axis, [(i, (i + by) % devices) for i in range(devices)])


def earlier_matrix(count):
    positions = jnp.arange(count, dtype=jnp.int32)
    return (positions[None, :] < positions[:, None]).astype(jnp.bfloat16)


def slot_ranks(route_block, experts):
    flat_routes = route_block.reshape(-1)
    hits = (flat_routes[:, None] == jnp.arange(experts, dtype=jnp.int32)[None, :]).astype(
        jnp.bfloat16
    )
    before = jnp.dot(earlier_matrix(flat_routes.shape[0]), hits, preferred_element_type=jnp.float32)
    ranks = jnp.sum(before * hits.astype(jnp.float32), axis=1).astype(jnp.int32)
    return ranks.reshape(route_block.shape)


def expert_ffn(slot_block, gate_matrix, up_matrix, down_matrix):
    gate_part = jnp.dot(slot_block, gate_matrix, preferred_element_type=jnp.float32)
    up_part = jnp.dot(slot_block, up_matrix, preferred_element_type=jnp.float32)
    hidden = (jax.nn.silu(gate_part) * up_part).astype(jnp.bfloat16)
    return jnp.dot(hidden, down_matrix, preferred_element_type=jnp.float32).astype(jnp.bfloat16)


def local(tokens, routes, norm_gain, router_weight, w_gate, w_up, w_down):
    local_rows = tokens[0]
    route_local = routes[0]
    gate_matrix = w_gate[0, 0]
    up_matrix = w_up[0, 0]
    down_matrix = w_down[0, 0]
    experts = lax.axis_size("expert")
    tok_dev, top_count = route_local.shape
    model_width = local_rows.shape[1]
    capacity = 3 * tok_dev * top_count // (2 * experts)
    wide_rows = local_rows.astype(jnp.float32)
    mean_square = jnp.mean(wide_rows * wide_rows, axis=-1, keepdims=True)
    normed = (wide_rows * lax.rsqrt(mean_square + 1e-06) * norm_gain[0]).astype(jnp.bfloat16)
    score = jax.nn.sigmoid(jnp.dot(normed, router_weight[0], preferred_element_type=jnp.float32))
    expert_ids = jnp.arange(experts, dtype=jnp.int32)
    chosen = route_local[..., None] == expert_ids[None, None, :]
    picked = jnp.sum(jnp.where(chosen, score[:, None, :], 0.0), axis=-1)
    gate_values = (picked / jnp.sum(picked, axis=1, keepdims=True)).astype(jnp.bfloat16)
    ranks = slot_ranks(route_local, experts)
    slots = route_local * capacity + ranks
    slot_hits = slots[..., None] == jnp.arange(experts * capacity, dtype=jnp.int32)[None, None, :]
    weights_map = jnp.sum(
        jnp.where(slot_hits, gate_values.astype(jnp.float32)[..., None], 0.0), axis=1
    ).astype(jnp.bfloat16)
    table = lax.all_gather(route_local, "expert", axis=0, tiled=True)
    gathered = lax.all_gather(normed, "expert", axis=0, tiled=True)
    own_index = lax.axis_index("expert")
    flat_count = tok_dev * top_count
    blocks = table.reshape(experts, flat_count)
    mine = blocks == own_index
    mine_values = mine.astype(jnp.bfloat16)
    own_ranks = jnp.dot(
        mine_values, earlier_matrix(flat_count).T, preferred_element_type=jnp.float32
    ).astype(jnp.int32)
    matches = mine[..., None] & (
        own_ranks[..., None] == jnp.arange(capacity, dtype=jnp.int32)[None, None, :]
    )
    selector = jnp.any(matches.reshape(experts, tok_dev, top_count, capacity), axis=2).astype(
        jnp.bfloat16
    )
    buffer = jnp.einsum(
        "btc,btd->bcd",
        selector,
        gathered.reshape(experts, tok_dev, model_width),
        preferred_element_type=jnp.float32,
    ).astype(jnp.bfloat16)
    owner_out = expert_ffn(buffer.reshape(-1, model_width), gate_matrix, up_matrix, down_matrix)
    returned = lax.all_to_all(
        owner_out.reshape(experts, capacity, model_width),
        "expert",
        split_axis=0,
        concat_axis=0,
        tiled=True,
    )
    moe = jnp.dot(
        weights_map,
        returned.reshape(experts * capacity, model_width),
        preferred_element_type=jnp.float32,
    )
    layer_out = (wide_rows + moe).astype(jnp.bfloat16)[None]
    received = shifted(layer_out, "pipe", 1)
    return received


def solution(mesh):
    return jax.shard_map(
        local,
        mesh=mesh,
        in_specs=(
            P("pipe", "expert", None),
            P("pipe", "expert", None),
            P("pipe", None),
            P("pipe", None, None),
            P("pipe", "expert", None, None),
            P("pipe", "expert", None, None),
            P("pipe", "expert", None, None),
        ),
        out_specs=P("pipe", "expert", None),
        check_vma=False,
    )
```

profile of v0, /device:TPU:2, one launch (start us, length us, event | category | flops | bytes accessed | tf_op | source)
XLA Modules:
  0.0 350.7 jit_solution(5233156969499989968)
XLA Ops:
  6.5 1.4 fusion.19
  7.9 2.0 fusion.21
  10.0 44.4 %all-gather = s32[1,4096,6]{1,0,2:T(1,128)S(1)} all-gather(s32[1,128,6]{1,0,2:T(1,128)} %param.8), channel_id=2, replica_groups=mesh['pipe'=8,'expert'=32] {'expert'}, dimensions={1}, use_global_device_ids=true | all-gather | bytes 101376 | tf_op jit(solution)/shard_map/all_gather | solution.py:58
  54.4 0.9 fusion.35
  55.3 1.5 copy.23
  56.8 2.5 eq.86
  59.3 1.0 fusion.14
  60.3 1.1 copy.24
  61.4 0.8 eq.87
  62.2 1.2 copy.25
  64.7 85.4 %all-gather.3.cloned.1.call-done = bf16[4096,2048]{1,0:T(8,128)(2,1)} async-done(((bf16[128,2048]{1,0:T(8,128)(2,1)}), bf16[4096,2048]{1,0:T(8,128)(2,1)}) %all-gather.3.cloned.1.call-update) | async-done | bytes 16777232 | tf_op jit(solution)/shard_map/all_gather | solution.py:59
  150.0 10.4 %convolution_convert_fusion.1 = bf16[32,36,2048]{2,1,0:T(8,128)(2,1)} fusion(bf16[32,128,2048]{2,1,0:T(8,128)(2,1)} %bitcast.55, pred[32,128,36]{1,0,2:T(8,128)(4,1)S(1)} %fusion.1), kind=kOutput, calls=%fused_computation.1 | convolution fusion | flops 606339072 | bytes 21643264 | tf_op jit(solution)/shard_map/btc,btd->bcd/dot_general | solution.py:74
  160.4 7.2 %reshape.90 = bf16[1152,2048]{1,0:T(8,128)(2,1)} reshape(bf16[32,36,2048]{2,1,0:T(8,128)(2,1)} %convolution_convert_fusion.1) | data formatting | bytes 9437184 | tf_op jit(solution)/shard_map/reshape | solution.py:80
  167.7 6.8 %fusion.5 = f32[1152,768]{1,0:T(8,128)S(1)} fusion(bf16[1152,2048]{1,0:T(8,128)(2,1)} %reshape.90, bf16[1,1,2048,768]{3,2,1,0:T(8,128)(2,1)} %param.11), kind=kOutput, calls=%fused_computation.11 | convolution fusion | flops 3623878656 | bytes 11403264 | tf_op jit(solution)/shard_map/dot_general | solution.py:28
  174.4 4.2 %fusion.2 = bf16[1152,768]{1,0:T(8,128)(2,1)S(1)} fusion(bf16[1152,2048]{1,0:T(8,128)(2,1)S(1)} %copy-done.1, f32[1152,768]{1,0:T(8,128)S(1)} %fusion.5, bf16[1,1,2048,768]{3,2,1,0:T(8,128)(2,1)S(1)} %copy-done.4), kind=kOutput, calls=%fused_computation.8 | convolution fusion | flops 3629187072 | bytes 13172736 | tf_op jit(solution)/shard_map/dot_general | solution.py:29
  178.6 5.5 %convolution_convert_fusion = bf16[1152,2048]{1,0:T(8,128)(2,1)} fusion(bf16[1152,768]{1,0:T(8,128)(2,1)S(1)} %fusion.2, bf16[1,1,768,2048]{3,2,1,0:T(8,128)(2,1)S(1)} %copy-done), kind=kOutput, calls=%fused_computation | convolution fusion | flops 3626237952 | bytes 9633792 | tf_op jit(solution)/shard_map/dot_general | solution.py:31
  184.2 7.2 %reshape.91 = bf16[32,36,2048]{2,1,0:T(8,128)(2,1)} reshape(bf16[1152,2048]{1,0:T(8,128)(2,1)} %convolution_convert_fusion) | data formatting | bytes 9437184 | tf_op jit(solution)/shard_map/reshape | solution.py:82
  191.4 5.8 %all-to-all-start = ((bf16[32,36,2048]{2,1,0:T(8,128)(2,1)}), bf16[32,36,2048]{2,1,0:T(8,128)(2,1)}, u32[]{:S(2)}, u32[]{:S(2)}) async-start(bf16[32,36,2048]{2,1,0:T(8,128)(2,1)} %reshape.91), calls=%async_computation | async-start | bytes 10485760 | tf_op jit(solution)/shard_map/all_to_all | solution.py:81
  198.1 1.5 fusion.18
  200.1 116.3 %all-to-all-done = bf16[32,36,2048]{2,1,0:T(8,128)(2,1)} async-done(((bf16[32,36,2048]{2,1,0:T(8,128)(2,1)}), bf16[32,36,2048]{2,1,0:T(8,128)(2,1)}, u32[]{:S(2)}, u32[]{:S(2)}) %all-to-all-start) | async-done | bytes 4718624 | tf_op jit(solution)/shard_map/all_to_all | solution.py:81
  316.4 7.2 %reshape.92 = bf16[1152,2048]{1,0:T(8,128)(2,1)} reshape(bf16[32,36,2048]{2,1,0:T(8,128)(2,1)} %all-to-all-done) | data formatting | bytes 9437184 | tf_op jit(solution)/shard_map/reshape | solution.py:90
  323.6 3.3 fusion.10
  326.9 1.6 collective-permute-start
  328.5 14.5 %collective-permute-done = bf16[1,128,2048]{2,1,0:T(8,128)(2,1)S(1)} collective-permute-done((bf16[1,128,2048]{2,1,0:T(8,128)(2,1)S(1)}, bf16[1,128,2048]{2,1,0:T(8,128)(2,1)S(1)}, u32[]{:S(2)}, u32[]{:S(2)}) %collective-permute-start) | collective-permute-done | bytes 524320 | tf_op jit(solution)/shard_map/ppermute | solution.py:9
  (27 shorter events, 3.5 us)
Async XLA Ops:
  6.5 172.1 %copy-start = (bf16[1,1,768,2048]{3,2,1,0:T(8,128)(2,1)S(1)}, bf16[1,1,768,2048]{3,2,1,0:T(8,128)(2,1)}, u32[]{:S(2)}) copy-start(bf16[1,1,768,2048]{3,2,1,0:T(8,128)(2,1)} %param.13) | copy-start | bytes 9437188
  6.5 143.5 %all-gather.3.cloned.1.call-start = ((), (), s32[]{:S(2)}) async-start(), calls=%async_computation.1 | async-start | bytes 17301504 | tf_op jit(solution)/shard_map/all_gather | solution.py:59
  167.7 6.8 %copy-start.1 = (bf16[1152,2048]{1,0:T(8,128)(2,1)S(1)}, bf16[1152,2048]{1,0:T(8,128)(2,1)}, u32[]{:S(2)}) copy-start(bf16[1152,2048]{1,0:T(8,128)(2,1)} %reshape.90) | copy-start | bytes 14155780
  167.7 6.8 %copy-start.4 = (bf16[1,1,2048,768]{3,2,1,0:T(8,128)(2,1)S(1)}, bf16[1,1,2048,768]{3,2,1,0:T(8,128)(2,1)}, u32[]{:S(2)}) copy-start(bf16[1,1,2048,768]{3,2,1,0:T(8,128)(2,1)} %param.12) | copy-start | bytes 9437188
  191.4 5.8 %copy-start.2 = (s32[1,128,6]{1,0,2:T(1,128)S(1)}, s32[1,128,6]{1,0,2:T(1,128)}, u32[]{:S(2)}) copy-start(s32[1,128,6]{1,0,2:T(1,128)} %param.8) | copy-start | bytes 9220
  191.4 6.7 %copy-start.3 = (f32[1,2048]{1,0:T(1,128)S(1)}, f32[1,2048]{1,0:T(1,128)}, u32[]{:S(2)}) copy-start(f32[1,2048]{1,0:T(1,128)} %param.9) | copy-start | bytes 24580
  191.4 125.0 %all-to-all-start = ((bf16[32,36,2048]{2,1,0:T(8,128)(2,1)}), bf16[32,36,2048]{2,1,0:T(8,128)(2,1)}, u32[]{:S(2)}, u32[]{:S(2)}) async-start(bf16[32,36,2048]{2,1,0:T(8,128)(2,1)} %reshape.91), calls=%async_computation | async-start | bytes 10485760 | tf_op jit(solution)/shard_map/all_to_all | solution.py:81
  326.9 16.1 %collective-permute-start = (bf16[1,128,2048]{2,1,0:T(8,128)(2,1)S(1)}, bf16[1,128,2048]{2,1,0:T(8,128)(2,1)S(1)}, u32[]{:S(2)}, u32[]{:S(2)}) collective-permute-start(bf16[1,128,2048]{2,1,0:T(8,128)(2,1)S(1)} %fusion.10), channel_id=1, source_target_pairs={{0,32},{32,64},{64,96},{96,128},{128,160},{160,192},{192,224},{224... | collective-permute-start | bytes 1572872 | tf_op jit(solution)/shard_map/ppermute | solution.py:9
Sparse Core Ops, SparseCore 0:
  10.1 139.8 all-gather.2
where the time goes:
time: 352 us; the launch traced here: 351 us
  waiting for transfers between devices  216 us (61%)
  blocking collectives  44.4 us (13%)
  matrix products  32.9 us (9%)
  local copies, waits for them, and re-layouts  30.8 us (9%)
  between operations  13.5 us (4%)
  starting transfers between devices  7.39 us (2%)
  other arithmetic  5.4 us (2%)
    all_to_all x1, waiting for transfers between devices, local(): lax.all_to_all(owner_out.reshape(experts, capacity, model_width), 'expert...  116 us
    all_gather x1, waiting for transfers between devices, local(): gathered = lax.all_gather(normed, 'expert', axis=0, tiled=True)  85.4 us
    all_gather x1, blocking collectives, local(): table = lax.all_gather(route_local, 'expert', axis=0, tiled=True)  44.4 us
    ppermute x1, waiting for transfers between devices, shifted(): lax.ppermute(shard, axis, [(i, (i + by) % devices) for i in range(devices)])  14.5 us
    dot_general x1, matrix products, local(): jnp.einsum('btc,btd->bcd', selector, gathered.reshape(experts, tok_dev, m...  10.4 us
    reshape x1, local copies, waits for them, and re-layouts, local(): buffer.reshape(-1, model_width)  7.24 us
    reshape x1, local copies, waits for them, and re-layouts, local(): returned.reshape(experts * capacity, model_width)  7.22 us
    reshape x1, local copies, waits for them, and re-layouts, local(): owner_out.reshape(experts, capacity, model_width)  7.21 us
  transfers between devices with their start and end apart: 3, of which 3 were waited for; matrix products, arithmetic and copies ran while one was open for 4% of the time, Pallas kernels for 0%

commit v1 on v0

--- a/solution.py
+++ b/solution.py
@@ -55,8 +55,13 @@
     weights_map = jnp.sum(
         jnp.where(slot_hits, gate_values.astype(jnp.float32)[..., None], 0.0), axis=1
     ).astype(jnp.bfloat16)
-    table = lax.all_gather(route_local, "expert", axis=0, tiled=True)
-    gathered = lax.all_gather(normed, "expert", axis=0, tiled=True)
+
+    def load_the_sources_all(obj, mat, which_axis="expert"):
+        last = jnp.concatenate([obj, mat], axis=1)
+        later = jax.lax.all_gather(last, which_axis, axis=0, tiled=True)
+        return jnp.split(later, [obj.shape[1]], axis=1)
+
+    table, gathered = load_the_sources_all(route_local, normed)
     own_index = lax.axis_index("expert")
     flat_count = tok_dev * top_count
     blocks = table.reshape(experts, flat_count)

time: 352 us -> 387 us (1.099)
  waiting for transfers between devices: 216 us -> 276 us
  blocking collectives: 44.4 us -> 0 us
  local copies, waits for them, and re-layouts: 30.8 us -> 48.6 us
    all_gather x1, waiting for transfers between devices: 85.4 us -> 145 us  [load_the_sources_all(): later = jax.lax.all_gather(last, which_axis, axis=0, tiled=True)]
    all_gather x1 -> x0, blocking collectives: 44.4 us -> none  [local(): table = lax.all_gather(route_local, 'expert', axis=0, tiled=True)]
    split x0 -> x1, local copies, waits for them, and re-layouts: none -> 17.6 us  [load_the_sources_all(): return jnp.split(later, [obj.shape[1]], axis=1)]
  transfers between devices with their start and end apart: 3 -> 3, of which waited for: 3 -> 3; matrix products, arithmetic and copies ran while one was open for 4% -> 1% of each run, Pallas kernels for 0% -> 0%
where the time goes in v1:
time: 387 us; the launch traced here: 386 us
  waiting for transfers between devices  276 us (71%)
  local copies, waits for them, and re-layouts  48.6 us (13%)
  matrix products  32.9 us (9%)
  between operations  13.6 us (4%)
  starting transfers between devices  7.6 us (2%)
  other arithmetic  7.04 us (2%)
    all_gather x1, waiting for transfers between devices, load_the_sources_all(): later = jax.lax.all_gather(last, which_axis, axis=0, tiled=True)  145 us
    all_to_all x1, waiting for transfers between devices, local(): lax.all_to_all(owner_out.reshape(experts, capacity, model_width), 'expert...  116 us
    split x1, local copies, waits for them, and re-layouts, load_the_sources_all(): return jnp.split(later, [obj.shape[1]], axis=1)  17.6 us
    ppermute x1, waiting for transfers between devices, shifted(): lax.ppermute(shard, axis, [(i, (i + by) % devices) for i in range(devices)])  14.5 us
    dot_general x1, matrix products, local(): jnp.einsum('btc,btd->bcd', selector, gathered.reshape(experts, tok_dev, m...  10.4 us
  transfers between devices with their start and end apart: 3, of which 3 were waited for; matrix products, arithmetic and copies ran while one was open for 1% of the time, Pallas kernels for 0%

profile of v1, /device:TPU:2, one launch (start us, length us, event | category | flops | bytes accessed | tf_op | source)
XLA Modules:
  0.0 385.7 jit_solution(15136146183871686570)
XLA Ops:
  6.5 1.4 fusion.19
  8.7 1.3 fusion.21
  10.0 1.0 pad_maximum_fusion
  11.1 145.1 %all-gather.2.cloned.1.call-done = bf16[4096,2054]{1,0:T(8,128)(2,1)} async-done(((bf16[128,2054]{1,0:T(8,128)(2,1)}), bf16[4096,2054]{1,0:T(8,128)(2,1)}) %all-gather.2.cloned.1.call-update) | async-done | bytes 16826384 | tf_op jit(solution)/shard_map/all_gather | solution.py:61
  156.2 2.3 slice_compare_fusion
  158.5 2.5 eq.86
  161.1 1.0 fusion.14
  162.1 1.1 copy.20
  164.0 1.2 copy.21
  165.2 1.7 copy.19
  167.4 17.6 %split.9 = bf16[4096,2048]{1,0:T(8,128)(2,1)} slice(bf16[4096,2054]{1,0:T(8,128)(2,1)} %all-gather.2.cloned.1.call-done), slice={[0:4096], [6:2054]} | slice | bytes 33554432 | tf_op jit(solution)/shard_map/split | solution.py:62
  185.0 10.4 %convolution_convert_fusion.1 = bf16[32,36,2048]{2,1,0:T(8,128)(2,1)} fusion(bf16[32,128,2048]{2,1,0:T(8,128)(2,1)} %bitcast.51, pred[32,128,36]{1,0,2:T(8,128)(4,1)S(1)} %fusion.1), kind=kOutput, calls=%fused_computation.1 | convolution fusion | flops 606339072 | bytes 21643264 | tf_op jit(solution)/shard_map/btc,btd->bcd/dot_general | solution.py:79
  195.4 7.2 %reshape.90 = bf16[1152,2048]{1,0:T(8,128)(2,1)} reshape(bf16[32,36,2048]{2,1,0:T(8,128)(2,1)} %convolution_convert_fusion.1) | data formatting | bytes 9437184 | tf_op jit(solution)/shard_map/reshape | solution.py:85
  202.6 6.8 %fusion.5 = f32[1152,768]{1,0:T(8,128)S(1)} fusion(bf16[1152,2048]{1,0:T(8,128)(2,1)} %reshape.90, bf16[1,1,2048,768]{3,2,1,0:T(8,128)(2,1)} %param.11), kind=kOutput, calls=%fused_computation.11 | convolution fusion | flops 3623878656 | bytes 11403264 | tf_op jit(solution)/shard_map/dot_general | solution.py:28
  209.4 4.2 %fusion.2 = bf16[1152,768]{1,0:T(8,128)(2,1)S(1)} fusion(bf16[1152,2048]{1,0:T(8,128)(2,1)S(1)} %copy-done.1, f32[1152,768]{1,0:T(8,128)S(1)} %fusion.5, bf16[1,1,2048,768]{3,2,1,0:T(8,128)(2,1)S(1)} %copy-done.6), kind=kOutput, calls=%fused_computation.8 | convolution fusion | flops 3629187072 | bytes 13172736 | tf_op jit(solution)/shard_map/dot_general | solution.py:29
  213.6 5.5 %convolution_convert_fusion = bf16[1152,2048]{1,0:T(8,128)(2,1)} fusion(bf16[1152,768]{1,0:T(8,128)(2,1)S(1)} %fusion.2, bf16[1,1,768,2048]{3,2,1,0:T(8,128)(2,1)S(1)} %copy-done), kind=kOutput, calls=%fused_computation | convolution fusion | flops 3626237952 | bytes 9633792 | tf_op jit(solution)/shard_map/dot_general | solution.py:31
  219.1 7.2 %reshape.91 = bf16[32,36,2048]{2,1,0:T(8,128)(2,1)} reshape(bf16[1152,2048]{1,0:T(8,128)(2,1)} %convolution_convert_fusion) | data formatting | bytes 9437184 | tf_op jit(solution)/shard_map/reshape | solution.py:87
  226.3 6.0 %all-to-all-start = ((bf16[32,36,2048]{2,1,0:T(8,128)(2,1)}), bf16[32,36,2048]{2,1,0:T(8,128)(2,1)}, u32[]{:S(2)}, u32[]{:S(2)}) async-start(bf16[32,36,2048]{2,1,0:T(8,128)(2,1)} %reshape.91), calls=%async_computation | async-start | bytes 10485760 | tf_op jit(solution)/shard_map/all_to_all | solution.py:86
  233.1 1.5 fusion.18
  235.2 116.2 %all-to-all-done = bf16[32,36,2048]{2,1,0:T(8,128)(2,1)} async-done(((bf16[32,36,2048]{2,1,0:T(8,128)(2,1)}), bf16[32,36,2048]{2,1,0:T(8,128)(2,1)}, u32[]{:S(2)}, u32[]{:S(2)}) %all-to-all-start) | async-done | bytes 4718624 | tf_op jit(solution)/shard_map/all_to_all | solution.py:86
  351.4 7.2 %reshape.92 = bf16[1152,2048]{1,0:T(8,128)(2,1)} reshape(bf16[32,36,2048]{2,1,0:T(8,128)(2,1)} %all-to-all-done) | data formatting | bytes 9437184 | tf_op jit(solution)/shard_map/reshape | solution.py:95
  358.6 3.3 fusion.10
  361.9 1.6 collective-permute-start
  363.5 14.5 %collective-permute-done = bf16[1,128,2048]{2,1,0:T(8,128)(2,1)S(1)} collective-permute-done((bf16[1,128,2048]{2,1,0:T(8,128)(2,1)S(1)}, bf16[1,128,2048]{2,1,0:T(8,128)(2,1)S(1)}, u32[]{:S(2)}, u32[]{:S(2)}) %collective-permute-start) | collective-permute-done | bytes 524320 | tf_op jit(solution)/shard_map/ppermute | solution.py:9
  (32 shorter events, 4.3 us)
Async XLA Ops:
  6.5 207.1 %copy-start = (bf16[1,1,768,2048]{3,2,1,0:T(8,128)(2,1)S(1)}, bf16[1,1,768,2048]{3,2,1,0:T(8,128)(2,1)}, u32[]{:S(2)}) copy-start(bf16[1,1,768,2048]{3,2,1,0:T(8,128)(2,1)} %param.13) | copy-start | bytes 9437188
  6.5 149.7 %all-gather.2.cloned.1.call-start = ((), (), s32[]{:S(2)}) async-start(), calls=%async_computation.1 | async-start | bytes 18382848 | tf_op jit(solution)/shard_map/all_gather | solution.py:61
  8.7 152.3 %copy-start.2 = (s32[1,128,6]{2,1,0:T(8,128)}, s32[1,128,6]{2,1,0:T(8,128)S(1)}, u32[]{:S(2)}) copy-start(s32[1,128,6]{2,1,0:T(8,128)S(1)} %copy.15) | copy-start | bytes 9220
  202.6 6.8 %copy-start.1 = (bf16[1152,2048]{1,0:T(8,128)(2,1)S(1)}, bf16[1152,2048]{1,0:T(8,128)(2,1)}, u32[]{:S(2)}) copy-start(bf16[1152,2048]{1,0:T(8,128)(2,1)} %reshape.90) | copy-start | bytes 14155780
  202.6 6.8 %copy-start.6 = (bf16[1,1,2048,768]{3,2,1,0:T(8,128)(2,1)S(1)}, bf16[1,1,2048,768]{3,2,1,0:T(8,128)(2,1)}, u32[]{:S(2)}) copy-start(bf16[1,1,2048,768]{3,2,1,0:T(8,128)(2,1)} %param.12) | copy-start | bytes 9437188
  226.3 6.0 %copy-start.4 = (s32[1,128,6]{1,0,2:T(1,128)S(1)}, s32[1,128,6]{1,0,2:T(1,128)}, u32[]{:S(2)}) copy-start(s32[1,128,6]{1,0,2:T(1,128)} %param.8) | copy-start | bytes 9220
  226.3 6.1 %copy-start.3 = (s32[1,128,6]{2,1,0:T(8,128)S(1)}, s32[1,128,6]{2,1,0:T(8,128)}, u32[]{:S(2)}) copy-start(s32[1,128,6]{2,1,0:T(8,128)} %copy-done.2) | copy-start | bytes 9220
  226.3 6.8 %copy-start.5 = (f32[1,2048]{1,0:T(1,128)S(1)}, f32[1,2048]{1,0:T(1,128)}, u32[]{:S(2)}) copy-start(f32[1,2048]{1,0:T(1,128)} %param.9) | copy-start | bytes 24580
  226.3 125.0 %all-to-all-start = ((bf16[32,36,2048]{2,1,0:T(8,128)(2,1)}), bf16[32,36,2048]{2,1,0:T(8,128)(2,1)}, u32[]{:S(2)}, u32[]{:S(2)}) async-start(bf16[32,36,2048]{2,1,0:T(8,128)(2,1)} %reshape.91), calls=%async_computation | async-start | bytes 10485760 | tf_op jit(solution)/shard_map/all_to_all | solution.py:86
  361.9 16.1 %collective-permute-start = (bf16[1,128,2048]{2,1,0:T(8,128)(2,1)S(1)}, bf16[1,128,2048]{2,1,0:T(8,128)(2,1)S(1)}, u32[]{:S(2)}, u32[]{:S(2)}) collective-permute-start(bf16[1,128,2048]{2,1,0:T(8,128)(2,1)S(1)} %fusion.10), channel_id=1, source_target_pairs={{0,32},{32,64},{64,96},{96,128},{128,160},{160,192},{192,224},{224... | collective-permute-start | bytes 1572872 | tf_op jit(solution)/shard_map/ppermute | solution.py:9
Sparse Core Ops, SparseCore 0:
  11.2 144.9 all-gather.1
